TPU v7x, 256 devices: a whole 4x4x8 slice. The times are simulated.
256 devices in a mesh: clip: 2 (over core), frame: 8 (over y, x_lo), band: 16 (over z, x_hi).
Axes of the slice: x: 4 (x_hi: 2, x_lo: 2; x = x_hi * 2 + x_lo), y: 4, z: 8, core: 2. Of those that a mesh axis runs over, the one named last changes fastest.
Arguments:
- latents: bfloat16 [4, 32, 64, 64, 320], P('clip', 'frame', 'band'), may hold values from -6 to 6
- spatial_kernel: bfloat16 [3, 3, 320, 320], replicated, may hold values from -0.109375 to 0.109375
- temporal_kernel: bfloat16 [3, 320, 320], replicated, may hold values from -0.1875 to 0.1875
- spatial_tangent: bfloat16 [3, 3, 320, 320], replicated, may hold values from -0.109375 to 0.109375
- temporal_tangent: bfloat16 [3, 320, 320], replicated, may hold values from -0.1875 to 0.1875
Outputs:
- curv_spatial: float32 [3, 3, 320, 320], replicated
- curv_temporal: float32 [3, 320, 320], replicated
All inputs are finite; a program needn't handle non-finite values.
Results may differ from a plain program's by a relative error of at most 0.00075.
Values may be sent and summed in bfloat16 or wider, within the bound.
No kernel may reach another device: no remote copies, remote signals or barrier semaphores. Data moves between devices by JAX's collectives and lax.ppermute only.
A program may use at most 128 MiB of HBM per device.

v0:
```python
import jax
import jax.numpy as jnp
from jax import lax
from jax.sharding import PartitionSpec as P


def padded_2(cells, sides, width):
    for axis, dim in sides:
        count = lax.axis_size(axis)
        ends = count - 1
        head = lax.slice_in_dim(cells, 0, width, axis=dim)
        tail = lax.slice_in_dim(cells, cells.shape[dim] - width, cells.shape[dim], axis=dim)
        cells = jnp.concatenate(
            [
                lax.ppermute(tail, axis, [(i, (i + 1) % count) for i in range(ends)]),
                cells,
                lax.ppermute(head, axis, [((i + 1) % count, i) for i in range(ends)]),
            ],
            axis=dim,
        )
    return cells


def forward_frames(framed, temporal_kernel, temporal_tangent):
    chans = framed.shape[-1]
    nframe = framed.shape[2] - 2
    act_pad = framed[0]
    dot_pad = framed[1]
    cat_act = jnp.concatenate([act_pad[:, k : k + nframe] for k in range(3)], axis=-1)
    cat_dot = jnp.concatenate([dot_pad[:, k : k + nframe] for k in range(3)], axis=-1)
    resid = jnp.einsum(
        "abrwk,kd->abrwd",
        cat_act,
        temporal_tangent.reshape(3 * chans, chans),
        preferred_element_type=jnp.float32,
    )
    resid = resid + jnp.einsum(
        "abrwk,kd->abrwd",
        cat_dot,
        temporal_kernel.reshape(3 * chans, chans),
        preferred_element_type=jnp.float32,
    )
    residual = resid.astype(jnp.bfloat16)
    grad_t = jnp.einsum("abrwk,abrwd->kd", cat_act, residual, preferred_element_type=jnp.float32)
    return (residual, grad_t)


def backward_frames(res_pad, temporal_kernel):
    nframe = res_pad.shape[1] - 2
    cat_res = jnp.concatenate([res_pad[:, 2 - k : 2 - k + nframe] for k in range(3)], axis=-1)
    back_w = jnp.concatenate([temporal_kernel[k].T for k in range(3)], axis=0)
    return jnp.einsum("abrwk,kd->abrwd", cat_res, back_w, preferred_element_type=jnp.float32)


def per_device(latents, spatial_kernel, temporal_kernel, spatial_tangent, temporal_tangent):
    chans = latents.shape[-1]
    rows = latents.shape[2]
    cols = latents.shape[3]
    padded = padded_2(latents, (("band", 2),), 1)
    padded = jnp.pad(padded, ((0, 0), (0, 0), (0, 0), (1, 1), (0, 0)))
    patches = jnp.concatenate(
        [padded[:, :, i : i + rows, j : j + cols, :] for i in range(3) for j in range(3)], axis=-1
    )
    both_w = jnp.concatenate(
        [spatial_kernel.reshape(9 * chans, chans), spatial_tangent.reshape(9 * chans, chans)],
        axis=1,
    )
    before = jnp.einsum("abrwk,kd->abrwd", patches, both_w, preferred_element_type=jnp.float32)
    hidden = before[..., :chans]
    tangent = before[..., chans:]
    sig = jax.nn.sigmoid(hidden)
    slope = sig * (1.0 + hidden * (1.0 - sig))
    active = (hidden * sig).astype(jnp.bfloat16)
    active_dot = (slope * tangent).astype(jnp.bfloat16)
    stacked = jnp.stack([active, active_dot])
    framed = padded_2(stacked, (("frame", 2),), 1)
    residual, grad_t = forward_frames(framed, temporal_kernel, temporal_tangent)
    res_pad = padded_2(residual, (("frame", 1),), 1)
    back = backward_frames(res_pad, temporal_kernel)
    hidden_bar = (slope * back).astype(jnp.bfloat16)
    grad_s = jnp.einsum("abrwk,abrwd->kd", patches, hidden_bar, preferred_element_type=jnp.float32)
    combined = jnp.concatenate(
        [grad_s.reshape(9, chans, chans), grad_t.reshape(3, chans, chans)], axis=0
    )
    total = lax.psum(combined, ("clip", "frame", "band"))
    devices = lax.axis_size("clip") * lax.axis_size("frame") * lax.axis_size("band")
    count = 1.0 * latents.shape[0] * latents.shape[1] * rows * cols * devices
    curv_spatial = (total[:9] * ((9.0 * chans) ** 0.5 / count)).reshape(3, 3, chans, chans)
    curv_temporal = total[9:] * ((3.0 * chans) ** 0.5 / count)
    return (curv_spatial, curv_temporal)


def solution(mesh):
    in_specs = (P("clip", "frame", "band", None, None), P(), P(), P(), P())
    out_specs = (P(), P())
    return jax.shard_map(
        per_device, mesh=mesh, in_specs=in_specs, out_specs=out_specs, check_vma=False
    )
```

profile of v0, /device:TPU:2, one launch (start us, length us, event | category | flops | bytes accessed | tf_op | source)
XLA Modules:
  0.0 461.5 jit_solution(8364531323663782129)
XLA Ops:
  8.5 4.1 collective-permute-start
  13.9 15.5 %collective-permute-done = bf16[2,4,1,64,320]{4,3,2,1,0:T(8,128)(2,1)S(1)} collective-permute-done((bf16[2,4,1,64,320]{4,3,2,1,0:T(8,128)(2,1)S(1)}, bf16[2,4,1,64,320]{4,3,2,1,0:T(8,128)(2,1)S(1)}, u32[]{:S(2)}, u32[]{:S(2)}) %collective-permute-start) | collective-permute-done | bytes 327712 | tf_op jit(solution)/shard_map/ppermute | solution.py:15
  29.3 2.4 fusion.23
  31.7 4.9 %fusion.46 = (bf16[2,4,4,64,320]{4,3,2,1,0:T(8,128)(2,1)}, bf16[2,4,4,64,320]{4,3,2,1,0:T(8,128)(2,1)}, bf16[2,4,4,64,320]{4,3,2,1,0:T(8,128)(2,1)}, bf16[2,4,4,...) fusion(bf16[2,4,6,66,320]{4,3,2,1,0:T(8,128)(2,1)S(1)} %fusion.23), kind=kLoop, calls=%fused_computation.61 | loop fusion | bytes 15728640 | tf_op jit(solution)/shard_map/slice | solution.py:62
  36.6 2.1 pad_maximum_fusion.5
  38.7 19.3 %concatenate.43 = bf16[2,4,4,64,2880]{4,3,2,1,0:T(8,128)(2,1)} concatenate(bf16[2,4,4,64,320]{4,3,2,1,0:T(8,128)(2,1)} %get-tuple-element.13, bf16[2,4,4,64,320]{4,3,2,1,0:T(8,128)(2,1)} %get-tuple-element.23, bf16[2,4,4,64,320]{4,3,2,1,0:T(8,128)(2,1)} %get-tuple-element.12, bf16[2,4,4,64,320]{4,3,2,1,0:T(8,128)(2,1)} %get-tuple-element.11, ...), dimensions={4} | concatenate | bytes 23592960 | tf_op jit(solution)/shard_map/concatenate | solution.py:61
  58.0 14.3 %fusion.15 = f32[2,4,4,64,640]{4,3,2,1,0:T(8,128)S(1)} fusion(bf16[2,4,4,64,2880]{4,3,2,1,0:T(8,128)(2,1)} %concatenate.43, bf16[2880,320]{1,0:T(8,128)(2,1)} %bitcast.56, bf16[2880,320]{1,0:T(8,128)(2,1)} %bitcast.57), kind=kOutput, calls=%fused_computation.22 | convolution fusion | flops 7557120000 | bytes 20725760 | tf_op jit(solution)/shard_map/abrwk,kd->abrwd/dot_general | solution.py:68
  72.3 1.5 fusion.30
  74.9 4.4 collective-permute-start.2
  79.2 2.1 collective-permute-start.3
  81.4 15.7 %collective-permute-done.2 = bf16[2,2,1,4,64,320]{5,4,3,2,1,0:T(8,128)(2,1)S(1)} collective-permute-done((bf16[2,2,1,4,64,320]{5,4,3,2,1,0:T(8,128)(2,1)S(1)}, bf16[2,2,1,4,64,320]{5,4,3,2,1,0:T(8,128)(2,1)S(1)}, u32[]{:S(2)}, u32[]{:S(2)}) %collective-permute-start.2) | collective-permute-done | bytes 655392 | tf_op jit(solution)/shard_map/ppermute | solution.py:15
  97.1 15.9 %collective-permute-done.3 = bf16[2,2,1,4,64,320]{5,4,3,2,1,0:T(8,128)(2,1)S(1)} collective-permute-done((bf16[2,2,1,4,64,320]{5,4,3,2,1,0:T(8,128)(2,1)S(1)}, bf16[2,2,1,4,64,320]{5,4,3,2,1,0:T(8,128)(2,1)S(1)}, u32[]{:S(2)}, u32[]{:S(2)}) %collective-permute-start.3) | collective-permute-done | bytes 655392 | tf_op jit(solution)/shard_map/ppermute | solution.py:17
  116.4 2.4 fusion.8
  118.8 2.7 add_convert_fusion
  121.6 3.3 collective-permute-start.4
  125.0 3.4 collective-permute-start.5
  128.4 2.8 fusion.31
  131.2 5.2 %collective-permute-done.4 = bf16[2,1,4,64,320]{4,3,2,1,0:T(8,128)(2,1)S(1)} collective-permute-done((bf16[2,1,4,64,320]{4,3,2,1,0:T(8,128)(2,1)S(1)}, bf16[2,1,4,64,320]{4,3,2,1,0:T(8,128)(2,1)S(1)}, u32[]{:S(2)}, u32[]{:S(2)}) %collective-permute-start.4) | collective-permute-done | bytes 327712 | tf_op jit(solution)/shard_map/ppermute | solution.py:17
  136.4 3.6 collective-permute-done.5
  140.8 17.6 %fusion.27 = f32[2880,320,1,1,1]{1,0,4,3,2:T(8,128)} fusion(bf16[2,4,4,64,2880]{4,3,2,1,0:T(8,128)(2,1)} %concatenate.43, bf16[2,4,4,64,320]{4,3,2,1,0:T(8,128)(2,1)} %copy-done.5, bf16[2,1,4,64,320]{4,3,2,1,0:T(8,128)(2,1)} %copy-done.6, bf16[2,1,4,64,320]{4,3,2,1,0:T(8,128)(2,1)S(1)} %collective-permute-done.4, ...), kind=kOutput, calls=%fused_computation.39 | convolution fusion | flops 5060567040 | bytes 21798912 | tf_op jit(solution)/shard_map/abrwk,abrwd->kd/dot_general | solution.py:81
  158.4 5.2 %pad_maximum_fusion = f32[12,320,320]{2,1,0:T(8,128)} fusion(f32[3,320,320]{2,1,0:T(8,128)S(1)} %bitcast.54, f32[9,320,320]{2,1,0:T(8,128)} %bitcast.52), kind=kLoop, calls=%fused_computation.2 | loop fusion | flops 1228800 | bytes 9830400 | tf_op jit(solution)/shard_map/concatenate | solution.py:82
  163.6 283.7 %all-reduce.3.cloned.1.call-done = f32[12,320,320]{2,1,0:T(8,128)} async-done(((f32[12,320,320]{2,1,0:T(8,128)}), f32[12,320,320]{2,1,0:T(8,128)}) %all-reduce.3.cloned.1.call-update) | async-done | bytes 4915216 | tf_op jit(solution)/shard_map/psum | solution.py:85
  447.3 4.8 %slice_multiply_fusion = f32[9,320,320]{2,1,0:T(8,128)} fusion(f32[12,320,320]{2,1,0:T(8,128)} %all-reduce.3.cloned.1.call-done), kind=kLoop, calls=%fused_computation.5 | loop fusion | flops 921600 | bytes 7372800 | tf_op jit(solution)/shard_map/mul | solution.py:88
  452.1 2.6 slice_multiply_fusion.2
  (25 shorter events, 7.9 us)
Async XLA Ops:
  7.2 111.7 %copy-start = (bf16[3,320,320]{2,1,0:T(8,128)(2,1)S(1)}, bf16[3,320,320]{2,1,0:T(8,128)(2,1)}, u32[]{:S(2)}) copy-start(bf16[3,320,320]{2,1,0:T(8,128)(2,1)} %param.9) | copy-start | bytes 1843204
  7.2 440.1 %all-reduce.3.cloned.1.call-start = ((), (), s32[]{:S(2)}) async-start(), calls=%async_computation | async-start | bytes 11796480 | tf_op jit(solution)/shard_map/psum | solution.py:85
  8.5 20.8 %collective-permute-start = (bf16[2,4,1,64,320]{4,3,2,1,0:T(8,128)(2,1)S(1)}, bf16[2,4,1,64,320]{4,3,2,1,0:T(8,128)(2,1)S(1)}, u32[]{:S(2)}, u32[]{:S(2)}) collective-permute-start(bf16[2,4,1,64,320]{4,3,2,1,0:T(8,128)(2,1)S(1)} %get-tuple-element.24), channel_id=1, source_target_pairs={{0,1},{1,2},{2,3},{3,4},{4,5},{5,6},{6,7},{7,8},{8,9},{9,10},{10,1... | collective-permute-start | bytes 983048 | tf_op jit(solution)/shard_map/ppermute | solution.py:15
  12.6 16.8 %collective-permute-start.1 = (bf16[2,4,1,64,320]{4,3,2,1,0:T(8,128)(2,1)S(1)}, bf16[2,4,1,64,320]{4,3,2,1,0:T(8,128)(2,1)S(1)}, u32[]{:S(2)}, u32[]{:S(2)}) collective-permute-start(bf16[2,4,1,64,320]{4,3,2,1,0:T(8,128)(2,1)S(1)} %get-tuple-element.25), channel_id=1, source_target_pairs={{1,0},{2,1},{3,2},{4,3},{5,4},{6,5},{7,6},{8,7},{9,8},{10,9},{11,1... | collective-permute-start | bytes 983048 | tf_op jit(solution)/shard_map/ppermute | solution.py:17
  31.7 4.9 %copy-start.2 = (bf16[2,4,4,64,320]{4,3,2,1,0:T(8,128)(2,1)S(1)}, bf16[2,4,4,64,320]{4,3,2,1,0:T(8,128)(2,1)}, u32[]{:S(2)}) copy-start(bf16[2,4,4,64,320]{4,3,2,1,0:T(8,128)(2,1)} %param.5) | copy-start | bytes 3932164
  72.3 2.3 copy-start.3
  74.6 6.8 %copy-start.4 = (bf16[3,320,320]{2,1,0:T(8,128)(2,1)S(1)}, bf16[3,320,320]{2,1,0:T(8,128)(2,1)}, u32[]{:S(2)}) copy-start(bf16[3,320,320]{2,1,0:T(8,128)(2,1)} %param.7) | copy-start | bytes 1843204
  74.9 22.3 %collective-permute-start.2 = (bf16[2,2,1,4,64,320]{5,4,3,2,1,0:T(8,128)(2,1)S(1)}, bf16[2,2,1,4,64,320]{5,4,3,2,1,0:T(8,128)(2,1)S(1)}, u32[]{:S(2)}, u32[]{:S(2)}) collective-permute-start(bf16[2,2,1,4,64,320]{5,4,3,2,1,0:T(8,128)(2,1)S(1)} %get-tuple-element.6), channel_id=1, source_target_pairs={{0,16},{16,32},{32,48},{48,64},{64,80},{80,96},{96,112},{1,17},{17... | collective-permute-start | bytes 1966088 | tf_op jit(solution)/shard_map/ppermute | solution.py:15
  79.2 33.8 %collective-permute-start.3 = (bf16[2,2,1,4,64,320]{5,4,3,2,1,0:T(8,128)(2,1)S(1)}, bf16[2,2,1,4,64,320]{5,4,3,2,1,0:T(8,128)(2,1)S(1)}, u32[]{:S(2)}, u32[]{:S(2)}) collective-permute-start(bf16[2,2,1,4,64,320]{5,4,3,2,1,0:T(8,128)(2,1)S(1)} %get-tuple-element.7), channel_id=1, source_target_pairs={{16,0},{32,16},{48,32},{64,48},{80,64},{96,80},{112,96},{17,1},{33... | collective-permute-start | bytes 1966088 | tf_op jit(solution)/shard_map/ppermute | solution.py:17
  121.5 9.7 %copy-start.5 = (bf16[2,4,4,64,320]{4,3,2,1,0:T(8,128)(2,1)}, bf16[2,4,4,64,320]{4,3,2,1,0:T(8,128)(2,1)S(1)}, u32[]{:S(2)}) copy-start(bf16[2,4,4,64,320]{4,3,2,1,0:T(8,128)(2,1)S(1)} %add_convert_fusion) | copy-start | bytes 3932164
  121.6 14.8 %collective-permute-start.4 = (bf16[2,1,4,64,320]{4,3,2,1,0:T(8,128)(2,1)S(1)}, bf16[2,1,4,64,320]{4,3,2,1,0:T(8,128)(2,1)S(1)}, u32[]{:S(2)}, u32[]{:S(2)}) collective-permute-start(bf16[2,1,4,64,320]{4,3,2,1,0:T(8,128)(2,1)S(1)} %get-tuple-element.20), channel_id=1, source_target_pairs={{16,0},{32,16},{48,32},{64,48},{80,64},{96,80},{112,96},{17,1},{33... | collective-permute-start | bytes 983048 | tf_op jit(solution)/shard_map/ppermute | solution.py:17
  125.0 15.1 %collective-permute-start.5 = (bf16[2,1,4,64,320]{4,3,2,1,0:T(8,128)(2,1)S(1)}, bf16[2,1,4,64,320]{4,3,2,1,0:T(8,128)(2,1)S(1)}, u32[]{:S(2)}, u32[]{:S(2)}) collective-permute-start(bf16[2,1,4,64,320]{4,3,2,1,0:T(8,128)(2,1)S(1)} %get-tuple-element.21), channel_id=1, source_target_pairs={{0,16},{16,32},{32,48},{48,64},{64,80},{80,96},{96,112},{1,17},{17... | collective-permute-start | bytes 983048 | tf_op jit(solution)/shard_map/ppermute | solution.py:15
  140.1 0.7 copy-start.6
  447.3 7.4 %copy-start.1 = (bf16[3,320,320]{2,1,0:T(8,128)(2,1)S(1)}, bf16[3,320,320]{2,1,0:T(8,128)(2,1)}, u32[]{:S(2)}) copy-start(bf16[3,320,320]{2,1,0:T(8,128)(2,1)} %param.9) | copy-start | bytes 1843204
Sparse Core Ops, SparseCore 0:
  163.8 283.4 all-reduce.2
where the time goes:
time: 463 us; the launch traced here: 462 us
  waiting for transfers between devices  340 us (73%)
  matrix products  39.7 us (9%)
  local copies, waits for them, and re-layouts  29.2 us (6%)
  other arithmetic  20.2 us (4%)
  starting transfers between devices  18.6 us (4%)
  between operations  14.2 us (3%)
    psum x1, waiting for transfers between devices, per_device(): total = lax.psum(combined, ('clip', 'frame', 'band'))  284 us
    ppermute x3, waiting for transfers between devices, padded_2(): lax.ppermute(tail, axis, [(i, (i + 1) % count) for i in range(ends)])  34.8 us
    ppermute x3, waiting for transfers between devices, padded_2(): lax.ppermute(head, axis, [((i + 1) % count, i) for i in range(ends)])  21.1 us
    concatenate x1, local copies, waits for them, and re-layouts, per_device(): jnp.concatenate([padded[:, :, i:i + rows, j:j + cols, :] for i in range(3...  19.3 us
    dot_general x1, matrix products, per_device(): jnp.einsum('abrwk,abrwd->kd', patches, hidden_bar, preferred_element_type...  17.6 us
    dot_general x1, matrix products, per_device(): jnp.einsum('abrwk,kd->abrwd', patches, both_w, preferred_element_type=jnp...  14.3 us
    ppermute x3, starting transfers between devices, padded_2(): lax.ppermute(tail, axis, [(i, (i + 1) % count) for i in range(ends)])  11.8 us
  transfers between devices with their start and end apart: 7, of which 6 were waited for; matrix products, arithmetic and copies ran while one was open for 1% of the time, Pallas kernels for 0%

commit v1 on v0

--- a/solution.py
+++ b/solution.py
@@ -2,6 +2,7 @@
 import jax.numpy as jnp
 from jax import lax
 from jax.sharding import PartitionSpec as P
+from jax.lax import psum
 
 
 def padded_2(cells, sides, width):
@@ -82,7 +83,11 @@
     combined = jnp.concatenate(
         [grad_s.reshape(9, chans, chans), grad_t.reshape(3, chans, chans)], axis=0
     )
-    total = lax.psum(combined, ("clip", "frame", "band"))
+
+    def proceed_the_point(device_axis, row_axis, local_block):
+        return psum(psum(local_block, device_axis), row_axis)
+
+    total = proceed_the_point(("frame", "band"), "clip", combined)
     devices = lax.axis_size("clip") * lax.axis_size("frame") * lax.axis_size("band")
     count = 1.0 * latents.shape[0] * latents.shape[1] * rows * cols * devices
     curv_spatial = (total[:9] * ((9.0 * chans) ** 0.5 / count)).reshape(3, 3, chans, chans)

time: 463 us -> 473 us (1.022)
  waiting for transfers between devices: 340 us -> 348 us
    psum x1 -> x2, waiting for transfers between devices: 284 us -> 292 us  [proceed_the_point(): return psum(psum(local_block, device_axis), row_axis)]
  transfers between devices with their start and end apart: 7 -> 8, of which waited for: 6 -> 7; matrix products, arithmetic and copies ran while one was open for 1% -> 1% of each run, Pallas kernels for 0% -> 0%
where the time goes in v1:
time: 473 us; the launch traced here: 470 us
  waiting for transfers between devices  348 us (74%)
  matrix products  39.7 us (8%)
  local copies, waits for them, and re-layouts  29.2 us (6%)
  other arithmetic  20.2 us (4%)
  starting transfers between devices  18.6 us (4%)
  between operations  14.2 us (3%)
    psum x2, waiting for transfers between devices, proceed_the_point(): return psum(psum(local_block, device_axis), row_axis)  292 us
    ppermute x3, waiting for transfers between devices, padded_2(): lax.ppermute(tail, axis, [(i, (i + 1) % count) for i in range(ends)])  34.8 us
    ppermute x3, waiting for transfers between devices, padded_2(): lax.ppermute(head, axis, [((i + 1) % count, i) for i in range(ends)])  21.1 us
    concatenate x1, local copies, waits for them, and re-layouts, per_device(): jnp.concatenate([padded[:, :, i:i + rows, j:j + cols, :] for i in range(3...  19.3 us
    dot_general x1, matrix products, per_device(): jnp.einsum('abrwk,abrwd->kd', patches, hidden_bar, preferred_element_type...  17.6 us
    dot_general x1, matrix products, per_device(): jnp.einsum('abrwk,kd->abrwd', patches, both_w, preferred_element_type=jnp...  14.3 us
    ppermute x3, starting transfers between devices, padded_2(): lax.ppermute(tail, axis, [(i, (i + 1) % count) for i in range(ends)])  11.8 us
  transfers between devices with their start and end apart: 8, of which 7 were waited for; matrix products, arithmetic and copies ran while one was open for 1% of the time, Pallas kernels for 0%

profile of v1, /device:TPU:2, one launch (start us, length us, event | category | flops | bytes accessed | tf_op | source)
XLA Modules:
  0.0 470.1 jit_solution(7393552117274042919)
XLA Ops:
  8.5 4.1 collective-permute-start
  13.9 15.5 %collective-permute-done = bf16[2,4,1,64,320]{4,3,2,1,0:T(8,128)(2,1)S(1)} collective-permute-done((bf16[2,4,1,64,320]{4,3,2,1,0:T(8,128)(2,1)S(1)}, bf16[2,4,1,64,320]{4,3,2,1,0:T(8,128)(2,1)S(1)}, u32[]{:S(2)}, u32[]{:S(2)}) %collective-permute-start) | collective-permute-done | bytes 327712 | tf_op jit(solution)/shard_map/ppermute | solution.py:16
  29.3 2.4 fusion.23
  31.7 4.9 %fusion.46 = (bf16[2,4,4,64,320]{4,3,2,1,0:T(8,128)(2,1)}, bf16[2,4,4,64,320]{4,3,2,1,0:T(8,128)(2,1)}, bf16[2,4,4,64,320]{4,3,2,1,0:T(8,128)(2,1)}, bf16[2,4,4,...) fusion(bf16[2,4,6,66,320]{4,3,2,1,0:T(8,128)(2,1)S(1)} %fusion.23), kind=kLoop, calls=%fused_computation.61 | loop fusion | bytes 15728640 | tf_op jit(solution)/shard_map/slice | solution.py:63
  36.6 2.1 pad_maximum_fusion.5
  38.7 19.3 %concatenate.43 = bf16[2,4,4,64,2880]{4,3,2,1,0:T(8,128)(2,1)} concatenate(bf16[2,4,4,64,320]{4,3,2,1,0:T(8,128)(2,1)} %get-tuple-element.13, bf16[2,4,4,64,320]{4,3,2,1,0:T(8,128)(2,1)} %get-tuple-element.23, bf16[2,4,4,64,320]{4,3,2,1,0:T(8,128)(2,1)} %get-tuple-element.12, bf16[2,4,4,64,320]{4,3,2,1,0:T(8,128)(2,1)} %get-tuple-element.11, ...), dimensions={4} | concatenate | bytes 23592960 | tf_op jit(solution)/shard_map/concatenate | solution.py:62
  58.0 14.3 %fusion.15 = f32[2,4,4,64,640]{4,3,2,1,0:T(8,128)S(1)} fusion(bf16[2,4,4,64,2880]{4,3,2,1,0:T(8,128)(2,1)} %concatenate.43, bf16[2880,320]{1,0:T(8,128)(2,1)} %bitcast.56, bf16[2880,320]{1,0:T(8,128)(2,1)} %bitcast.57), kind=kOutput, calls=%fused_computation.22 | convolution fusion | flops 7557120000 | bytes 20725760 | tf_op jit(solution)/shard_map/abrwk,kd->abrwd/dot_general | solution.py:69
  74.9 4.4 collective-permute-start.2
  79.2 2.1 collective-permute-start.3
  81.4 15.7 %collective-permute-done.2 = bf16[2,2,1,4,64,320]{5,4,3,2,1,0:T(8,128)(2,1)S(1)} collective-permute-done((bf16[2,2,1,4,64,320]{5,4,3,2,1,0:T(8,128)(2,1)S(1)}, bf16[2,2,1,4,64,320]{5,4,3,2,1,0:T(8,128)(2,1)S(1)}, u32[]{:S(2)}, u32[]{:S(2)}) %collective-permute-start.2) | collective-permute-done | bytes 655392 | tf_op jit(solution)/shard_map/ppermute | solution.py:16
  97.1 15.9 %collective-permute-done.3 = bf16[2,2,1,4,64,320]{5,4,3,2,1,0:T(8,128)(2,1)S(1)} collective-permute-done((bf16[2,2,1,4,64,320]{5,4,3,2,1,0:T(8,128)(2,1)S(1)}, bf16[2,2,1,4,64,320]{5,4,3,2,1,0:T(8,128)(2,1)S(1)}, u32[]{:S(2)}, u32[]{:S(2)}) %collective-permute-start.3) | collective-permute-done | bytes 655392 | tf_op jit(solution)/shard_map/ppermute | solution.py:18
  116.4 2.4 fusion.8
  118.8 2.7 add_convert_fusion
  121.6 3.3 collective-permute-start.4
  125.0 3.4 collective-permute-start.5
  128.4 2.8 fusion.31
  131.2 5.2 %collective-permute-done.4 = bf16[2,1,4,64,320]{4,3,2,1,0:T(8,128)(2,1)S(1)} collective-permute-done((bf16[2,1,4,64,320]{4,3,2,1,0:T(8,128)(2,1)S(1)}, bf16[2,1,4,64,320]{4,3,2,1,0:T(8,128)(2,1)S(1)}, u32[]{:S(2)}, u32[]{:S(2)}) %collective-permute-start.4) | collective-permute-done | bytes 327712 | tf_op jit(solution)/shard_map/ppermute | solution.py:18
  136.4 3.6 collective-permute-done.5
  140.8 17.6 %fusion.27 = f32[2880,320,1,1,1]{1,0,4,3,2:T(8,128)} fusion(bf16[2,4,4,64,2880]{4,3,2,1,0:T(8,128)(2,1)} %concatenate.43, bf16[2,4,4,64,320]{4,3,2,1,0:T(8,128)(2,1)} %copy-done.5, bf16[2,1,4,64,320]{4,3,2,1,0:T(8,128)(2,1)} %copy-done.6, bf16[2,1,4,64,320]{4,3,2,1,0:T(8,128)(2,1)S(1)} %collective-permute-done.4, ...), kind=kOutput, calls=%fused_computation.39 | convolution fusion | flops 5060567040 | bytes 21798912 | tf_op jit(solution)/shard_map/abrwk,abrwd->kd/dot_general | solution.py:82
  158.4 5.2 %pad_maximum_fusion = f32[12,320,320]{2,1,0:T(8,128)} fusion(f32[3,320,320]{2,1,0:T(8,128)S(1)} %bitcast.54, f32[9,320,320]{2,1,0:T(8,128)} %bitcast.52), kind=kLoop, calls=%fused_computation.2 | loop fusion | flops 1228800 | bytes 9830400 | tf_op jit(solution)/shard_map/concatenate | solution.py:83
  163.7 250.9 %all-reduce.4.cloned.1.call-done = f32[12,320,320]{2,1,0:T(8,128)} async-done(((f32[12,320,320]{2,1,0:T(8,128)}), f32[12,320,320]{2,1,0:T(8,128)}) %all-reduce.4.cloned.1.call-update) | async-done | bytes 4915216 | tf_op jit(solution)/shard_map/psum | solution.py:88
  414.6 41.3 %all-reduce.6.cloned.1.call-done = f32[12,320,320]{2,1,0:T(8,128)} async-done(((f32[12,320,320]{2,1,0:T(8,128)}), f32[12,320,320]{2,1,0:T(8,128)}) %all-reduce.6.cloned.1.call-update) | async-done | bytes 4915216 | tf_op jit(solution)/shard_map/psum | solution.py:88
  455.9 4.8 %slice_multiply_fusion = f32[9,320,320]{2,1,0:T(8,128)} fusion(f32[12,320,320]{2,1,0:T(8,128)} %all-reduce.6.cloned.1.call-done), kind=kLoop, calls=%fused_computation.5 | loop fusion | flops 921600 | bytes 7372800 | tf_op jit(solution)/shard_map/mul | solution.py:93
  460.6 2.6 slice_multiply_fusion.2
  (28 shorter events, 9.5 us)
Async XLA Ops:
  7.2 111.7 %copy-start = (bf16[3,320,320]{2,1,0:T(8,128)(2,1)S(1)}, bf16[3,320,320]{2,1,0:T(8,128)(2,1)}, u32[]{:S(2)}) copy-start(bf16[3,320,320]{2,1,0:T(8,128)(2,1)} %param.9) | copy-start | bytes 1843204
  7.2 407.4 %all-reduce.4.cloned.1.call-start = ((), (), s32[]{:S(2)}) async-start(), calls=%async_computation | async-start | bytes 11796480 | tf_op jit(solution)/shard_map/psum | solution.py:88
  8.5 20.8 %collective-permute-start = (bf16[2,4,1,64,320]{4,3,2,1,0:T(8,128)(2,1)S(1)}, bf16[2,4,1,64,320]{4,3,2,1,0:T(8,128)(2,1)S(1)}, u32[]{:S(2)}, u32[]{:S(2)}) collective-permute-start(bf16[2,4,1,64,320]{4,3,2,1,0:T(8,128)(2,1)S(1)} %get-tuple-element.24), channel_id=1, source_target_pairs={{0,1},{1,2},{2,3},{3,4},{4,5},{5,6},{6,7},{7,8},{8,9},{9,10},{10,1... | collective-permute-start | bytes 983048 | tf_op jit(solution)/shard_map/ppermute | solution.py:16
  12.6 16.8 %collective-permute-start.1 = (bf16[2,4,1,64,320]{4,3,2,1,0:T(8,128)(2,1)S(1)}, bf16[2,4,1,64,320]{4,3,2,1,0:T(8,128)(2,1)S(1)}, u32[]{:S(2)}, u32[]{:S(2)}) collective-permute-start(bf16[2,4,1,64,320]{4,3,2,1,0:T(8,128)(2,1)S(1)} %get-tuple-element.25), channel_id=1, source_target_pairs={{1,0},{2,1},{3,2},{4,3},{5,4},{6,5},{7,6},{8,7},{9,8},{10,9},{11,1... | collective-permute-start | bytes 983048 | tf_op jit(solution)/shard_map/ppermute | solution.py:18
  31.7 4.9 %copy-start.2 = (bf16[2,4,4,64,320]{4,3,2,1,0:T(8,128)(2,1)S(1)}, bf16[2,4,4,64,320]{4,3,2,1,0:T(8,128)(2,1)}, u32[]{:S(2)}) copy-start(bf16[2,4,4,64,320]{4,3,2,1,0:T(8,128)(2,1)} %param.5) | copy-start | bytes 3932164
  72.3 2.3 copy-start.3
  74.6 6.8 %copy-start.4 = (bf16[3,320,320]{2,1,0:T(8,128)(2,1)S(1)}, bf16[3,320,320]{2,1,0:T(8,128)(2,1)}, u32[]{:S(2)}) copy-start(bf16[3,320,320]{2,1,0:T(8,128)(2,1)} %param.7) | copy-start | bytes 1843204
  74.9 22.3 %collective-permute-start.2 = (bf16[2,2,1,4,64,320]{5,4,3,2,1,0:T(8,128)(2,1)S(1)}, bf16[2,2,1,4,64,320]{5,4,3,2,1,0:T(8,128)(2,1)S(1)}, u32[]{:S(2)}, u32[]{:S(2)}) collective-permute-start(bf16[2,2,1,4,64,320]{5,4,3,2,1,0:T(8,128)(2,1)S(1)} %get-tuple-element.6), channel_id=1, source_target_pairs={{0,16},{16,32},{32,48},{48,64},{64,80},{80,96},{96,112},{1,17},{17... | collective-permute-start | bytes 1966088 | tf_op jit(solution)/shard_map/ppermute | solution.py:16
  79.2 33.8 %collective-permute-start.3 = (bf16[2,2,1,4,64,320]{5,4,3,2,1,0:T(8,128)(2,1)S(1)}, bf16[2,2,1,4,64,320]{5,4,3,2,1,0:T(8,128)(2,1)S(1)}, u32[]{:S(2)}, u32[]{:S(2)}) collective-permute-start(bf16[2,2,1,4,64,320]{5,4,3,2,1,0:T(8,128)(2,1)S(1)} %get-tuple-element.7), channel_id=1, source_target_pairs={{16,0},{32,16},{48,32},{64,48},{80,64},{96,80},{112,96},{17,1},{33... | collective-permute-start | bytes 1966088 | tf_op jit(solution)/shard_map/ppermute | solution.py:18
  121.5 9.7 %copy-start.5 = (bf16[2,4,4,64,320]{4,3,2,1,0:T(8,128)(2,1)}, bf16[2,4,4,64,320]{4,3,2,1,0:T(8,128)(2,1)S(1)}, u32[]{:S(2)}) copy-start(bf16[2,4,4,64,320]{4,3,2,1,0:T(8,128)(2,1)S(1)} %add_convert_fusion) | copy-start | bytes 3932164
  121.6 14.8 %collective-permute-start.4 = (bf16[2,1,4,64,320]{4,3,2,1,0:T(8,128)(2,1)S(1)}, bf16[2,1,4,64,320]{4,3,2,1,0:T(8,128)(2,1)S(1)}, u32[]{:S(2)}, u32[]{:S(2)}) collective-permute-start(bf16[2,1,4,64,320]{4,3,2,1,0:T(8,128)(2,1)S(1)} %get-tuple-element.20), channel_id=1, source_target_pairs={{16,0},{32,16},{48,32},{64,48},{80,64},{96,80},{112,96},{17,1},{33... | collective-permute-start | bytes 983048 | tf_op jit(solution)/shard_map/ppermute | solution.py:18
  125.0 15.1 %collective-permute-start.5 = (bf16[2,1,4,64,320]{4,3,2,1,0:T(8,128)(2,1)S(1)}, bf16[2,1,4,64,320]{4,3,2,1,0:T(8,128)(2,1)S(1)}, u32[]{:S(2)}, u32[]{:S(2)}) collective-permute-start(bf16[2,1,4,64,320]{4,3,2,1,0:T(8,128)(2,1)S(1)} %get-tuple-element.21), channel_id=1, source_target_pairs={{0,16},{16,32},{32,48},{48,64},{64,80},{80,96},{96,112},{1,17},{17... | collective-permute-start | bytes 983048 | tf_op jit(solution)/shard_map/ppermute | solution.py:16
  140.1 0.7 copy-start.6
  163.6 292.2 %all-reduce.6.cloned.1.call-start = ((), (), s32[]{:S(2)}) async-start(), calls=%async_computation.1 | async-start | bytes 11796480 | tf_op jit(solution)/shard_map/psum | solution.py:88
  455.9 7.4 %copy-start.1 = (bf16[3,320,320]{2,1,0:T(8,128)(2,1)S(1)}, bf16[3,320,320]{2,1,0:T(8,128)(2,1)}, u32[]{:S(2)}) copy-start(bf16[3,320,320]{2,1,0:T(8,128)(2,1)} %param.9) | copy-start | bytes 1843204
Sparse Core Ops, SparseCore 0:
  163.8 250.7 all-reduce.3
  417.3 38.4 all-reduce.5
